TPU v7x, 128 devices: a whole 4x4x4 slice. The times are simulated.
128 devices in a mesh: gx: 8 (over z, y_hi), gy: 16 (over x, y_lo, core).
Axes of the slice: x: 4, y: 4 (y_hi: 2, y_lo: 2; y = y_hi * 2 + y_lo), z: 4, core: 2. Of those that a mesh axis runs over, the one named last changes fastest.
Arguments:
- interior_inverse: bfloat16 [16, 16, 1536, 1536], P('gx', 'gy'), as said below
- coupling: bfloat16 [16, 16, 1536, 1024], P('gx', 'gy'), may hold values from -0.15625 to 0.15625
- face_stiffness: bfloat16 [16, 16, 4, 256, 256], P('gx', 'gy'), as said below
- corner_basis: bfloat16 [16, 16, 24, 1024], P('gx', 'gy'), may hold values from -0.25 to 0.25
- loads: float32 [16, 16, 4, 256], P('gx', 'gy'), may hold values from -48 to 48
- face_order: int32 [16, 16, 4, 256], P('gx', 'gy'), may hold values from 0 to 255, each once within a row
- corner_index: int32 [16, 16, 24], P('gx', 'gy'), may hold values from 0 to 1791, as said below
- coarse_inverse: float32 [1792, 1792], P(None, ('gx', 'gy')), as said below
Outputs:
- solution: float32 [16, 16, 4, 256], P('gx', 'gy')
- residual: float32 [16, 16, 4, 256], P('gx', 'gy')
Inputs may be any that keep to these rules, and one draw needn't show every extreme that they name: `interior_inverse`: symmetric positive definite. `face_stiffness`: each block is symmetric, and every subdomain's interface Schur complement is positive definite. `corner_index`: subdomains that share a grid vertex give its 6 coarse dofs the same indices in the same order (corners in the order top-left, top-right, bottom-left, bottom-right); the 24 indices of a subdomain are distinct; distinct vertices have distinct indices. `coarse_inverse`: symmetric positive definite.
All inputs are finite; a program needn't handle non-finite values.
Results may differ from a plain program's by a relative error of at most 0.01.
Values sent between devices are 32-bit elements; how exact they have to be, the bound alone decides.
No kernel may reach another device: no remote copies, remote signals or barrier semaphores. Data moves between devices by JAX's collectives and lax.ppermute only.
A program may use at most 128 MiB of HBM per device.

v0:
```python
import jax
import jax.numpy as jnp
from jax import lax
from jax.sharding import Mesh
from jax.sharding import PartitionSpec as P

ITERS = 2
GX = ("gx_0", "gx_1")
GY = ("gy_0", "gy_1", "gy_2")
GX_GY = ("gx_0", "gx_1", "gy_0", "gy_1", "gy_2")
careful = lax.Precision.HIGHEST


def from_behind(value, axis, steps):
    count = lax.axis_size(axis)
    first, last = (max(0, -steps), min(count, count - steps))
    return lax.ppermute(value, axis, [(source, source + steps) for source in range(first, last)])


def by_axis(array, axes):
    for axis in axes:
        array = lax.psum(array, axis)
    return array


def inverse_order(ordering):
    extent = ordering.shape[-1]
    levels = jnp.arange(extent, dtype=jnp.int32)
    matches = ordering[..., :, None] == levels
    return jnp.sum(jnp.where(matches, levels[:, None], 0), axis=-2)


def reorder(values, positions):
    return jnp.take_along_axis(values, positions, axis=-1)


def permute_block(matrix, ordering):
    extent = ordering.shape[-1]
    levels = jnp.arange(extent, dtype=jnp.int32)
    picker = (ordering[..., None, :] == levels[:, None]).astype(jnp.float32)
    rows_done = jnp.einsum("sfgk,sfkl->sfgl", picker, matrix, precision=careful)
    return jnp.einsum("sfgl,sfhl->sfgh", rows_done, picker, precision=careful)


def invert(summed):
    factor_low = jnp.linalg.cholesky(summed)
    identity = jnp.broadcast_to(jnp.eye(summed.shape[-1], dtype=jnp.float32), summed.shape)
    factor = lax.linalg.triangular_solve(factor_low, identity, left_side=True, lower=True)
    return jnp.einsum("...ik,...il->...kl", factor, factor, precision=careful)


def half_inner(first, second):
    return 0.5 * jnp.sum(first * second)


def swap_vectors(vector_in):
    from_above = from_behind(vector_in[-1, 1], GX, 1)
    from_below = from_behind(vector_in[0, 0], GX, -1)
    from_west = from_behind(vector_in[:, 3], GY, 1)
    from_east = from_behind(vector_in[:, 2], GY, -1)
    north_side = jnp.concatenate([from_above[None], vector_in[:-1, 1]], axis=0)
    south_side = jnp.concatenate([vector_in[1:, 0], from_below[None]], axis=0)
    return jnp.stack([north_side, south_side, from_west, from_east], axis=1)


def shards(
    interior_inverse,
    coupling,
    face_stiffness,
    corner_basis,
    loads,
    face_order,
    corner_index,
    coarse_inverse,
):
    local_count = interior_inverse.shape[0]
    inner_dofs = interior_inverse.shape[2]
    face_dofs = loads.shape[3]
    inverse_mat = interior_inverse.reshape(local_count, inner_dofs, inner_dofs)
    couple = coupling.reshape(local_count, inner_dofs, 4 * face_dofs)
    couple_faces = couple.reshape(local_count, inner_dofs, 4, face_dofs)
    stiffness = face_stiffness.reshape(local_count, 4, face_dofs, face_dofs)
    basis = corner_basis.reshape(local_count, corner_basis.shape[2], 4 * face_dofs)
    basis_wide = basis.astype(jnp.float32)
    ordering = face_order.reshape(local_count, 4, face_dofs)
    backward = inverse_order(ordering)
    corners = corner_index.reshape(local_count, corner_index.shape[2])
    coarse_total = coarse_inverse.shape[0]
    row_ids = lax.axis_index(GX) * local_count + jnp.arange(local_count, dtype=jnp.int32)
    col_id = lax.axis_index(GY)
    row_total = local_count * lax.axis_size(GX)
    col_total = lax.axis_size(GY)
    west_live = jnp.broadcast_to(col_id > 0, (local_count,))
    east_live = jnp.broadcast_to(col_id < col_total - 1, (local_count,))
    live_mask = jnp.stack(
        [row_ids > 0, row_ids < row_total - 1, west_live, east_live], axis=1
    ).astype(jnp.float32)[:, :, None]
    products = jnp.einsum(
        "sij,sjk->sik", inverse_mat, couple, preferred_element_type=jnp.float32
    ).astype(jnp.bfloat16)
    product_faces = products.reshape(local_count, inner_dofs, 4, face_dofs)
    schur_local = stiffness.astype(jnp.float32) - jnp.einsum(
        "sifk,sifl->sfkl", couple_faces, product_faces, preferred_element_type=jnp.float32
    )
    schur_canon = permute_block(schur_local, ordering)
    partner = from_behind(schur_canon[0, 0], GX, -1)
    partner_south = jnp.concatenate([schur_canon[1:, 0], partner[None]], axis=0)
    partner_side = from_behind(schur_canon[:, 2], GY, -1)
    south_inverse = invert(schur_canon[:, 1] + partner_south)
    east_inverse = invert(schur_canon[:, 3] + partner_side)
    top_inverse = from_behind(south_inverse[-1], GX, 1)
    north_inverse = jnp.concatenate([top_inverse[None], south_inverse[:-1]], axis=0)
    west_inverse = from_behind(east_inverse, GY, 1)
    face_inverse = jnp.stack([north_inverse, south_inverse, west_inverse, east_inverse], axis=1)
    loads_canon = reorder(loads.reshape(local_count, 4, face_dofs), backward)
    residual = live_mask * (loads_canon + swap_vectors(loads_canon))
    solution = jnp.zeros_like(residual)
    search = jnp.zeros_like(residual)
    along = jnp.zeros_like(residual)
    gamma_old = jnp.float32(1.0)
    alpha_old = jnp.float32(1.0)
    for iteration in range(ITERS):
        smoothed = jnp.einsum("sfkl,sfl->sfk", face_inverse, residual, precision=careful)
        share = jnp.einsum("sfkl,sfl->sfk", schur_canon, smoothed, precision=careful)
        share_local = (
            reorder(share, ordering).astype(jnp.bfloat16).reshape(local_count, 4 * face_dofs)
        )
        corner_res = jnp.einsum(
            "sjk,sk->sj", basis, share_local, preferred_element_type=jnp.float32
        )
        matches = (corners[:, :, None] == jnp.arange(coarse_total, dtype=jnp.int32)).astype(
            jnp.float32
        )
        dense = jnp.einsum("sj,sjg->g", corner_res, matches, precision=careful)
        owned = lax.psum_scatter(dense, GX_GY, scatter_dimension=0, tiled=True)
        partial_sol = jnp.dot(coarse_inverse, owned, precision=careful)
        coarse_sol = by_axis(partial_sol, GX_GY)
        corner_sol = jnp.einsum("sjg,g->sj", matches, coarse_sol, precision=careful)
        lifted = jnp.einsum("sjk,sj->sk", basis_wide, corner_sol, precision=careful).reshape(
            local_count, 4, face_dofs
        )
        spread = jnp.einsum(
            "sfkl,sfl->sfk", schur_canon, reorder(lifted, backward), precision=careful
        )
        precond_out = live_mask * jnp.einsum(
            "sfkl,sfl->sfk",
            face_inverse,
            residual + spread + swap_vectors(spread),
            precision=careful,
        )
        plain = reorder(precond_out, ordering).astype(jnp.bfloat16)
        middle = jnp.einsum(
            "sik,sk->si",
            couple,
            plain.reshape(local_count, 4 * face_dofs),
            preferred_element_type=jnp.float32,
        ).astype(jnp.bfloat16)
        solved = jnp.einsum(
            "sij,sj->si", inverse_mat, middle, preferred_element_type=jnp.float32
        ).astype(jnp.bfloat16)
        direct = jnp.einsum("sfkl,sfl->sfk", stiffness, plain, preferred_element_type=jnp.float32)
        back_part = jnp.einsum(
            "sifk,si->sfk", couple_faces, solved, preferred_element_type=jnp.float32
        )
        canon_out = reorder(direct - back_part, backward)
        image = live_mask * (canon_out + swap_vectors(canon_out))
        gamma, delta = (
            by_axis(half_inner(residual, precond_out), GX_GY),
            by_axis(half_inner(precond_out, image), GX_GY),
        )
        if iteration == 0:
            alpha = gamma / delta
            search = precond_out
            along = image
        else:
            beta = gamma / gamma_old
            alpha = gamma / (delta - beta * gamma / alpha_old)
            search = precond_out + beta * search
            along = image + beta * along
        solution = solution + alpha * search
        residual = residual - alpha * along
        gamma_old = gamma
        alpha_old = alpha
    return (
        solution.reshape(local_count, 1, 4, face_dofs),
        residual.reshape(local_count, 1, 4, face_dofs),
    )


def solution(mesh):
    torus = Mesh(mesh.devices.reshape(4, 2, 4, 2, 2), ("gx_0", "gx_1", "gy_0", "gy_1", "gy_2"))
    in_specs = (
        P(GX, GY, None, None),
        P(GX, GY, None, None),
        P(GX, GY, None, None, None),
        P(GX, GY, None, None),
        P(GX, GY, None, None),
        P(GX, GY, None, None),
        P(GX, GY, None),
        P(None, GX_GY),
    )
    out_specs = (P(GX, GY, None, None), P(GX, GY, None, None))
    return jax.shard_map(
        shards, mesh=torus, in_specs=in_specs, out_specs=out_specs, check_vma=False
    )
```

profile of v0, /device:TPU:1, one launch (start us, length us, event | category | flops | bytes accessed | tf_op | source)
XLA Modules:
  0.0 947.1 jit_solution(5315609379234085832)
XLA Ops:
  0.6 11.2 %reshape_reshape.3 = bf16[2,1536,4,256]{3,2,1,0:T(4,128)(2,1)} reshape(bf16[2,1,1536,1024]{3,2,1,0:T(8,128)(2,1)} %param.14) | data formatting | bytes 12582912 | tf_op jit(solution)/shard_map/reshape;reshape | solution.py:81
  11.9 16.5 %fusion.11 = bf16[2,1536,1024]{1,2,0:T(8,128)(2,1)} fusion(bf16[2,1,1536,1024]{3,2,1,0:T(8,128)(2,1)} %param.14, bf16[2,1,1536,1536]{3,2,1,0:T(8,128)(2,1)} %param.13), kind=kOutput, calls=%fused_computation.24 | convolution fusion | flops 9666822144 | bytes 22020096 | tf_op jit(solution)/shard_map/sij,sjk->sik/dot_general | solution.py:98
  28.9 6.4 fusion.20
  48.4 20.4 %gather_fusion = f32[2048]{0:T(1024)S(1)} fusion(f32[2,4,256]{2,1,0:T(4,128)S(1)} %bitcast.383, s32[2048]{0:T(1024)S(1)} %bitcast.390), kind=kCustom, calls=%fused_computation.clone | custom fusion | bytes 40960 | tf_op jit(solution)/shard_map/jit(take_along_axis)/gather | solution.py:34
  70.1 6.3 collective-permute-start
  103.6 23.5 %custom-call.36 = f32[2,128,128]{2,1,0:T(8,128)S(1)} custom-call(f32[2,128,128]{2,1,0:T(8,128)S(1)} %cholesky.198), custom_call_target="Cholesky" | custom-call | tf_op jit(solution)/shard_map/jit(cholesky)/cholesky | solution.py:46
  134.8 24.3 %custom-call.40 = f32[2,128,128]{2,1,0:T(8,128)S(1)} custom-call(f32[2,128,128]{2,1,0:T(8,128)} %cholesky.201), custom_call_target="Cholesky" | custom-call | tf_op jit(solution)/shard_map/jit(cholesky)/cholesky | solution.py:46
  160.5 21.1 %custom-call.37 = f32[2,1,128,128]{2,3,1,0:T(8,128)} custom-call(f32[2,1,128,128]{3,2,1,0:T(8,128)} %get-tuple-element.99), custom_call_target="InvertDiagBlocksLowerTriangular" | custom-call | tf_op jit(solution)/shard_map/jit(cholesky)/cholesky | solution.py:46
  185.4 25.0 %custom-call.38 = f32[2,128,128]{2,1,0:T(8,128)} custom-call(f32[2,128,128]{2,1,0:T(8,128)} %convolution_subtract_fusion.2), custom_call_target="Cholesky" | custom-call | tf_op jit(solution)/shard_map/jit(cholesky)/cholesky | solution.py:46
  210.5 21.1 %custom-call.41 = f32[2,1,128,128]{2,3,1,0:T(8,128)} custom-call(f32[2,1,128,128]{3,2,1,0:T(8,128)} %get-tuple-element.100), custom_call_target="InvertDiagBlocksLowerTriangular" | custom-call | tf_op jit(solution)/shard_map/jit(cholesky)/cholesky | solution.py:46
  236.2 24.9 %custom-call.42 = f32[2,128,128]{2,1,0:T(8,128)} custom-call(f32[2,128,128]{2,1,0:T(8,128)} %slice_subtract_fusion), custom_call_target="Cholesky" | custom-call | tf_op jit(solution)/shard_map/jit(cholesky)/cholesky | solution.py:46
  267.1 8.7 while.4
  275.8 40.9 %custom-call.39 = f32[2,2,128,128]{2,3,1,0:T(8,128)} custom-call(f32[2,2,128,128]{3,2,1,0:T(8,128)} %bitcast.412), custom_call_target="InvertDiagBlocksLowerTriangular" | custom-call | tf_op jit(solution)/shard_map/triangular_solve/custom-call.0 | solution.py:48
  323.3 8.7 while.5
  332.1 40.7 %custom-call.43 = f32[2,2,128,128]{2,3,1,0:T(8,128)} custom-call(f32[2,2,128,128]{3,2,1,0:T(8,128)} %bitcast.411), custom_call_target="InvertDiagBlocksLowerTriangular" | custom-call | tf_op jit(solution)/shard_map/triangular_solve/custom-call.0 | solution.py:48
  381.7 6.4 collective-permute-start.5
  397.3 21.2 %gather_fusion.1 = bf16[2048]{0:T(1024)(128)(2,1)S(1)} fusion(bf16[2,4,256]{2,1,0:T(4,128)(2,1)S(1)} %bitcast.384, s32[2048]{0:T(1024)S(1)} %bitcast.386), kind=kCustom, calls=%fused_computation.1.clone | custom fusion | bytes 32768 | tf_op jit(solution)/shard_map/jit(take_along_axis)/gather | solution.py:34
  419.0 73.2 %all-reduce.1 = f32[1792]{0:T(1024)S(1)} all-reduce(f32[1792]{0:T(1024)S(1)} %convolution_reduce_fusion.3), channel_id=2, replica_groups=mesh['gx_0'=4,'gx_1'=2,'gy_0'=4,'gy_1'=2,'gy_2'=2] {'gx_0','gx_1','gy_0'..., use_global_device_ids=true, to_apply=%region_5.0.clone | all-reduce | flops 1792 | bytes 14336
  492.5 7.6 psum.210
  500.1 5.4 psum.211
  505.4 7.3 psum.212
  516.6 9.1 psum.214
  526.5 20.4 %gather_fusion.2 = f32[2048]{0:T(1024)S(1)} fusion(f32[2,4,256]{2,1,0:T(4,128)S(1)} %reshape.122, s32[2048]{0:T(1024)S(1)} %bitcast.393), kind=kCustom, calls=%fused_computation.2.clone | custom fusion | bytes 40960 | tf_op jit(solution)/shard_map/jit(take_along_axis)/gather | solution.py:34
  563.5 20.4 %gather_fusion.3 = bf16[2048]{0:T(1024)(128)(2,1)S(1)} fusion(f32[2,4,256]{2,1,0:T(4,128)S(1)} %bitcast_multiply_fusion.1, s32[2048]{0:T(1024)S(1)} %bitcast.387), kind=kCustom, calls=%fused_computation.3.clone | custom fusion | bytes 32768 | tf_op jit(solution)/shard_map/jit(take_along_axis)/gather | solution.py:34
  588.6 6.4 fusion.2
  596.4 20.4 %gather_fusion.4 = f32[2048]{0:T(1024)S(1)} fusion(f32[2,4,256]{2,1,0:T(4,128)S(1)} %bitcast_subtract_fusion.3, s32[2048]{0:T(1024)S(1)} %bitcast.391), kind=kCustom, calls=%fused_computation.4.clone | custom fusion | bytes 40960 | tf_op jit(solution)/shard_map/jit(take_along_axis)/gather | solution.py:34
  616.8 6.4 collective-permute-start.12
  633.4 10.4 %all-reduce.6 = (f32[]{:T(128)}, f32[]{:T(128)}) all-reduce(f32[]{:T(128)S(6)} %mul.109, f32[]{:T(128)S(6)} %mul.112), channel_id=1, replica_groups=mesh['gx_0'=4,'gx_1'=2,'gy_0'=4,'gy_1'=2,'gy_2'=2] {'gx_0'}, use_global_device_ids=true, to_apply=%region_12.0 | all-reduce | flops 2 | bytes 16 | tf_op jit(solution)/shard_map/psum | solution.py:22
  643.8 5.9 all-reduce.12
  649.7 7.2 all-reduce.4
  656.8 6.0 all-reduce.10
  662.9 8.7 all-reduce.8
  678.2 20.8 %gather_fusion.5 = bf16[2048]{0:T(1024)(128)(2,1)S(1)} fusion(bf16[2,4,256]{2,1,0:T(4,128)(2,1)S(1)} %bitcast.385, s32[2048]{0:T(1024)S(1)} %bitcast.388), kind=kCustom, calls=%fused_computation.5.clone | custom fusion | bytes 32768 | tf_op jit(solution)/shard_map/jit(take_along_axis)/gather | solution.py:34
  699.5 61.9 %all-reduce.2 = f32[1792]{0:T(1024)S(1)} all-reduce(f32[1792]{0:T(1024)S(1)} %convolution_reduce_fusion.2), channel_id=3, replica_groups=mesh['gx_0'=4,'gx_1'=2,'gy_0'=4,'gy_1'=2,'gy_2'=2] {'gx_0','gx_1','gy_0'..., use_global_device_ids=true, to_apply=%region_23.0.clone | all-reduce | flops 1792 | bytes 14336
  761.7 7.9 psum.225
  769.6 5.4 psum.226
  774.9 7.0 psum.227
  785.7 9.1 psum.229
  795.7 20.4 %gather_fusion.6 = f32[2048]{0:T(1024)S(1)} fusion(f32[2,4,256]{2,1,0:T(4,128)S(1)} %reshape.125, s32[2048]{0:T(1024)S(1)} %bitcast.394), kind=kCustom, calls=%fused_computation.6.clone | custom fusion | bytes 40960 | tf_op jit(solution)/shard_map/jit(take_along_axis)/gather | solution.py:34
  832.1 20.4 %gather_fusion.7 = bf16[2048]{0:T(1024)(128)(2,1)S(1)} fusion(f32[2,4,256]{2,1,0:T(4,128)S(1)} %bitcast_multiply_fusion, s32[2048]{0:T(1024)S(1)} %bitcast.389), kind=kCustom, calls=%fused_computation.7.clone | custom fusion | bytes 32768 | tf_op jit(solution)/shard_map/jit(take_along_axis)/gather | solution.py:34
  857.2 6.4 fusion
  864.9 20.4 %gather_fusion.8 = f32[2048]{0:T(1024)S(1)} fusion(f32[2,4,256]{2,1,0:T(4,128)S(1)} %bitcast_subtract_fusion.2, s32[2048]{0:T(1024)S(1)} %bitcast.392), kind=kCustom, calls=%fused_computation.8.clone | custom fusion | bytes 40960 | tf_op jit(solution)/shard_map/jit(take_along_axis)/gather | solution.py:34
  885.4 6.4 collective-permute-start.20
  902.1 10.9 %all-reduce.5 = (f32[]{:T(128)}, f32[]{:T(128)}) all-reduce(f32[]{:T(128)S(6)} %mul.118, f32[]{:T(128)S(6)} %mul.121), channel_id=1, replica_groups=mesh['gx_0'=4,'gx_1'=2,'gy_0'=4,'gy_1'=2,'gy_2'=2] {'gx_0'}, use_global_device_ids=true, to_apply=%region_30.0 | all-reduce | flops 2 | bytes 16 | tf_op jit(solution)/shard_map/psum | solution.py:22
  913.0 6.0 all-reduce.11
  918.9 7.9 all-reduce.3
  926.8 5.3 all-reduce.9
  932.1 8.8 all-reduce.7
  (308 shorter events, 187.1 us)
Async XLA Ops:
  0.6 491.6 %copy-start = (f32[1792,14]{0,1:T(8,128)S(1)}, f32[1792,14]{0,1:T(8,128)}, u32[]{:S(2)}) copy-start(f32[1792,14]{0,1:T(8,128)} %param.20) | copy-start | bytes 301060
  11.9 16.5 %copy-start.2 = (bf16[2,1,4,256,256]{4,3,2,1,0:T(8,128)(2,1)S(1)}, bf16[2,1,4,256,256]{4,3,2,1,0:T(8,128)(2,1)}, u32[]{:S(2)}) copy-start(bf16[2,1,4,256,256]{4,3,2,1,0:T(8,128)(2,1)} %param.15) | copy-start | bytes 3145732
  39.9 57.4 %collective-permute-start.4 = (f32[256,256]{0,1:T(8,128)}, f32[256,256]{0,1:T(8,128)}, u32[]{:S(2)}, u32[]{:S(2)}) collective-permute-start(f32[256,256]{0,1:T(8,128)} %bitcast.410), channel_id=1, source_target_pairs={{16,0},{32,16},{48,32},{64,48},{80,64},{96,80},{112,96},{17,1},{33... | collective-permute-start | bytes 786440 | tf_op jit(solution)/shard_map/ppermute | solution.py:17
  44.6 83.3 %collective-permute-start.6 = (f32[2,256,256]{1,2,0:T(8,128)}, f32[2,256,256]{1,2,0:T(8,128)}, u32[]{:S(2)}, u32[]{:S(2)}) collective-permute-start(f32[2,256,256]{1,2,0:T(8,128)} %bitcast.409), channel_id=1, source_target_pairs={{1,0},{2,1},{3,2},{4,3},{5,4},{6,5},{7,6},{8,7},{9,8},{10,9},{11,1... | collective-permute-start | bytes 1572872 | tf_op jit(solution)/shard_map/ppermute | solution.py:17
  48.3 20.5 %copy-start.19 = (s32[2,4,256]{2,1,0:T(4,128)}, s32[2,4,256]{2,1,0:T(4,128)S(1)}, u32[]{:S(2)}) copy-start(s32[2,4,256]{2,1,0:T(4,128)S(1)} %select_reduce_fusion) | copy-start | bytes 24580
  70.1 24.0 %collective-permute-start = (f32[256]{0:T(256)}, f32[256]{0:T(256)}, u32[]{:S(2)}, u32[]{:S(2)}) collective-permute-start(f32[256]{0:T(256)} %bitcast.3), channel_id=1, source_target_pairs={{0,16},{16,32},{32,48},{48,64},{64,80},{80,96},{96,112},{1,17},{17... | collective-permute-start | bytes 3080 | tf_op jit(solution)/shard_map/ppermute | solution.py:17
  76.3 311.7 %collective-permute-start.1 = (f32[256]{0:T(256)}, f32[256]{0:T(256)}, u32[]{:S(2)}, u32[]{:S(2)}) collective-permute-start(f32[256]{0:T(256)} %bitcast.7), channel_id=1, source_target_pairs={{16,0},{32,16},{48,32},{64,48},{80,64},{96,80},{112,96},{17,1},{33... | collective-permute-start | bytes 3080 | tf_op jit(solution)/shard_map/ppermute | solution.py:17
  78.2 310.5 %collective-permute-start.2 = (f32[2,256]{1,0:T(2,128)}, f32[2,256]{1,0:T(2,128)}, u32[]{:S(2)}, u32[]{:S(2)}) collective-permute-start(f32[2,256]{1,0:T(2,128)} %get-tuple-element.129), channel_id=1, source_target_pairs={{0,1},{1,2},{2,3},{3,4},{4,5},{5,6},{6,7},{7,8},{8,9},{9,10},{10,1... | collective-permute-start | bytes 6152 | tf_op jit(solution)/shard_map/ppermute | solution.py:17
  94.1 295.3 %collective-permute-start.3 = (f32[2,256]{1,0:T(2,128)}, f32[2,256]{1,0:T(2,128)}, u32[]{:S(2)}, u32[]{:S(2)}) collective-permute-start(f32[2,256]{1,0:T(2,128)} %get-tuple-element.130), channel_id=1, source_target_pairs={{1,0},{2,1},{3,2},{4,3},{5,4},{6,5},{7,6},{8,7},{9,8},{10,9},{11,1... | collective-permute-start | bytes 6152 | tf_op jit(solution)/shard_map/ppermute | solution.py:17
  262.9 53.8 %copy-start.9 = (f32[128,256]{1,0:T(8,128)S(1)}, f32[128,256]{1,0:T(8,128)}, u32[]{:S(2)}) copy-start(f32[128,256]{1,0:T(8,128)} %get-tuple-element.94) | copy-start | bytes 393220
  263.2 54.8 %copy-start.8 = (f32[128,256]{1,0:T(8,128)S(1)}, f32[128,256]{1,0:T(8,128)}, u32[]{:S(2)}) copy-start(f32[128,256]{1,0:T(8,128)} %get-tuple-element.93) | copy-start | bytes 393220
  372.8 15.2 %copy-start.26 = (f32[1,256]{1,0:T(1,128)S(1)}, f32[1,256]{1,0:T(1,128)}, u32[]{:S(2)}) copy-start(f32[1,256]{1,0:T(1,128)} %get-tuple-element.127) | copy-start | bytes 3076
  372.8 15.9 %copy-start.25 = (f32[2,256]{1,0:T(2,128)S(1)}, f32[2,256]{1,0:T(2,128)}, u32[]{:S(2)}) copy-start(f32[2,256]{1,0:T(2,128)} %pad_maximum_fusion.1) | copy-start | bytes 6148
  372.8 17.2 %copy-start.21 = (f32[2,4]{1,0:T(2,128)S(1)}, f32[2,4]{1,0:T(2,128)}, u32[]{:S(2)}) copy-start(f32[2,4]{1,0:T(2,128)} %add_convert_fusion) | copy-start | bytes 100
  378.0 17.4 %copy-start.10 = (f32[2,256,256]{2,1,0:T(8,128)}, f32[2,256,256]{2,1,0:T(8,128)S(1)}, u32[]{:S(2)}) copy-start(f32[2,256,256]{2,1,0:T(8,128)S(1)} %fusion.44) | copy-start | bytes 1572868
  378.0 15.5 %collective-permute-start.7 = (f32[2,256,256]{2,1,0:T(8,128)S(1)}, f32[2,256,256]{2,1,0:T(8,128)S(1)}, u32[]{:S(2)}, u32[]{:S(2)}) collective-permute-start(f32[2,256,256]{2,1,0:T(8,128)S(1)} %fusion.44), channel_id=1, source_target_pairs={{0,1},{1,2},{2,3},{3,4},{4,5},{5,6},{6,7},{7,8},{8,9},{9,10},{10,1... | collective-permute-start | bytes 1572872 | tf_op jit(solution)/shard_map/ppermute | solution.py:17
  381.7 11.8 %collective-permute-start.5 = (f32[256,256]{1,0:T(8,128)S(1)}, f32[256,256]{1,0:T(8,128)S(1)}, u32[]{:S(2)}, u32[]{:S(2)}) collective-permute-start(f32[256,256]{1,0:T(8,128)S(1)} %get-tuple-element.91), channel_id=1, source_target_pairs={{0,16},{16,32},{32,48},{48,64},{64,80},{80,96},{96,112},{1,17},{17... | collective-permute-start | bytes 786440 | tf_op jit(solution)/shard_map/ppermute | solution.py:17
  397.2 21.2 %copy-start.18 = (s32[2,1,4,256]{3,2,1,0:T(4,128)S(1)}, s32[2,1,4,256]{3,2,1,0:T(4,128)}, u32[]{:S(2)}) copy-start(s32[2,1,4,256]{3,2,1,0:T(4,128)} %param.18) | copy-start | bytes 24580
  397.3 21.3 %copy-start.16 = (bf16[2,1,24,1024]{3,2,1,0:T(8,128)(2,1)S(1)}, bf16[2,1,24,1024]{3,2,1,0:T(8,128)(2,1)}, u32[]{:S(2)}) copy-start(bf16[2,1,24,1024]{3,2,1,0:T(8,128)(2,1)} %param.16) | copy-start | bytes 294916
  397.3 21.4 %copy-start.30 = (s32[2,1,24]{2,1,0:T(1,128)S(1)}, s32[2,1,24]{2,1,0:T(1,128)}, u32[]{:S(2)}) copy-start(s32[2,1,24]{2,1,0:T(1,128)} %param.19) | copy-start | bytes 580
  526.5 20.5 %copy-start.20 = (s32[2,4,256]{2,1,0:T(4,128)S(1)}, s32[2,4,256]{2,1,0:T(4,128)}, u32[]{:S(2)}) copy-start(s32[2,4,256]{2,1,0:T(4,128)} %copy-done.19) | copy-start | bytes 24580
  546.9 14.6 %copy-start.22 = (f32[2,4]{1,0:T(2,128)S(1)}, f32[2,4]{1,0:T(2,128)}, u32[]{:S(2)}) copy-start(f32[2,4]{1,0:T(2,128)} %add_convert_fusion) | copy-start | bytes 100
  547.0 14.6 %copy-start.4 = (f32[2,256,256]{2,1,0:T(8,128)S(1)}, f32[2,256,256]{2,1,0:T(8,128)}, u32[]{:S(2)}) copy-start(f32[2,256,256]{2,1,0:T(8,128)} %fusion.40) | copy-start | bytes 1572868
  547.0 14.6 %copy-start.11 = (f32[2,256,256]{2,1,0:T(8,128)S(1)}, f32[2,256,256]{2,1,0:T(8,128)}, u32[]{:S(2)}) copy-start(f32[2,256,256]{2,1,0:T(8,128)} %copy-done.10) | copy-start | bytes 1572868
  547.0 14.6 %copy-start.14 = (f32[2,1,256,256]{3,2,0,1:T(8,128)S(1)}, f32[2,1,256,256]{3,2,0,1:T(8,128)}, u32[]{:S(2)}) copy-start(f32[2,1,256,256]{3,2,0,1:T(8,128)} %copy-done.13) | copy-start | bytes 1572868
  547.0 14.6 %copy-start.28 = (f32[2,256,256]{2,1,0:T(8,128)S(1)}, f32[2,256,256]{2,1,0:T(8,128)}, u32[]{:S(2)}) copy-start(f32[2,256,256]{2,1,0:T(8,128)} %copy-done.27) | copy-start | bytes 1572868
  548.9 9.6 %collective-permute-start.8 = (f32[256]{0:T(256)S(1)}, f32[256]{0:T(256)S(1)}, u32[]{:S(2)}, u32[]{:S(2)}) collective-permute-start(f32[256]{0:T(256)S(1)} %bitcast.451), channel_id=1, source_target_pairs={{0,16},{16,32},{32,48},{48,64},{64,80},{80,96},{96,112},{1,17},{17... | collective-permute-start | bytes 3080 | tf_op jit(solution)/shard_map/ppermute | solution.py:17
  551.7 6.8 collective-permute-start.9
  553.0 5.6 collective-permute-start.10
  556.6 4.9 collective-permute-start.11
  583.9 11.1 %slice-start = ((s8[6291456]{0:T(1024)(128)(4,1)}), s8[4194304]{0:T(1024)(128)(4,1)S(1)}, s32[]{:S(2)}) async-start(s8[6291456]{0:T(1024)(128)(4,1)} %bitcast.395), calls=%async_computation | async-start | bytes 8388608
  596.4 20.5 %copy-start.23 = (pred[2,4,256]{2,0,1:T(4,128)(4,1)S(1)}, pred[2,4,256]{2,0,1:T(4,128)(4,1)}, u32[]{:S(2)}) copy-start(pred[2,4,256]{2,0,1:T(4,128)(4,1)} %get-tuple-element.81) | copy-start | bytes 6148
  616.8 12.0 %collective-permute-start.12 = (f32[256]{0:T(256)S(1)}, f32[256]{0:T(256)S(1)}, u32[]{:S(2)}, u32[]{:S(2)}) collective-permute-start(f32[256]{0:T(256)S(1)} %bitcast.452), channel_id=1, source_target_pairs={{0,16},{16,32},{32,48},{48,64},{64,80},{80,96},{96,112},{1,17},{17... | collective-permute-start | bytes 3080 | tf_op jit(solution)/shard_map/ppermute | solution.py:17
  623.2 5.8 collective-permute-start.13
  624.5 4.5 collective-permute-start.14
  626.5 4.9 collective-permute-start.15
  816.1 14.0 %copy-start.5 = (f32[2,256,256]{2,1,0:T(8,128)S(1)}, f32[2,256,256]{2,1,0:T(8,128)}, u32[]{:S(2)}) copy-start(f32[2,256,256]{2,1,0:T(8,128)} %fusion.40) | copy-start | bytes 1572868
  816.1 14.0 %copy-start.12 = (f32[2,256,256]{2,1,0:T(8,128)S(1)}, f32[2,256,256]{2,1,0:T(8,128)}, u32[]{:S(2)}) copy-start(f32[2,256,256]{2,1,0:T(8,128)} %copy-done.10) | copy-start | bytes 1572868
  816.1 14.0 %copy-start.15 = (f32[2,1,256,256]{3,2,0,1:T(8,128)S(1)}, f32[2,1,256,256]{3,2,0,1:T(8,128)}, u32[]{:S(2)}) copy-start(f32[2,1,256,256]{3,2,0,1:T(8,128)} %copy-done.13) | copy-start | bytes 1572868
  816.2 14.0 %copy-start.29 = (f32[2,256,256]{2,1,0:T(8,128)S(1)}, f32[2,256,256]{2,1,0:T(8,128)}, u32[]{:S(2)}) copy-start(f32[2,256,256]{2,1,0:T(8,128)} %copy-done.27) | copy-start | bytes 1572868
  818.1 9.3 collective-permute-start.16
  820.6 6.8 collective-permute-start.17
  821.9 5.6 collective-permute-start.18
  825.2 4.9 collective-permute-start.19
  885.4 12.0 %collective-permute-start.20 = (f32[256]{0:T(256)S(1)}, f32[256]{0:T(256)S(1)}, u32[]{:S(2)}, u32[]{:S(2)}) collective-permute-start(f32[256]{0:T(256)S(1)} %bitcast.454), channel_id=1, source_target_pairs={{0,16},{16,32},{32,48},{48,64},{64,80},{80,96},{96,112},{1,17},{17... | collective-permute-start | bytes 3080 | tf_op jit(solution)/shard_map/ppermute | solution.py:17
  891.8 5.8 collective-permute-start.21
  893.1 4.5 collective-permute-start.22
  895.1 5.0 collective-permute-start.23
  (12 other events, 66.9 us)
where the time goes:
time: 958 us; the launch traced here: 947 us
  blocking collectives  278 us (29%)
  other arithmetic  246 us (26%)
  local copies, waits for them, and re-layouts  239 us (25%)
  matrix products  88.5 us (9%)
  starting transfers between devices  70.9 us (7%)
  waiting for transfers between devices  13.9 us (1%)
  between operations  10.7 us (1%)
    gather x19, local copies, waits for them, and re-layouts, reorder(): return jnp.take_along_axis(values, positions, axis=-1)  185 us
    another operation x14, other arithmetic, invert(): factor_low = jnp.linalg.cholesky(summed)  145 us
    psum x20, blocking collectives, by_axis(): array = lax.psum(array, axis)  143 us
    unnamed x2, blocking collectives  135 us
    another operation x5, other arithmetic, invert(): lax.linalg.triangular_solve(factor_low, identity, left_side=True, lower=T...  85.3 us
    ppermute x24, starting transfers between devices, from_behind(): lax.ppermute(value, axis, [(source, source + steps) for source in range(f...  70.9 us
    another operation x16, local copies, waits for them, and re-layouts, invert(): lax.linalg.triangular_solve(factor_low, identity, left_side=True, lower=T...  20.3 us
  transfers between devices with their start and end apart: 24, of which 7 were waited for; matrix products, arithmetic and copies ran while one was open for 34% of the time, Pallas kernels for 0%

commit v1 on v0

--- a/solution.py
+++ b/solution.py
@@ -19,7 +19,7 @@
 
 def by_axis(array, axes):
     for axis in axes:
-        array = lax.psum(array, axis)
+        array = jnp.sum(lax.all_gather(array, axis), axis=0)
     return array
 
 

time: 958 us -> 1000 us (1.044)
  local copies, waits for them, and re-layouts: 239 us -> 267 us
  other arithmetic: 246 us -> 258 us
    psum x20 -> x0, blocking collectives: 143 us -> none  [by_axis(): array = lax.psum(array, axis)]
    unnamed x2 -> x12, blocking collectives: 135 us -> 209 us
    all_gather x0 -> x10, blocking collectives: none -> 72.6 us  [by_axis(): array = jnp.sum(lax.all_gather(array, axis), axis=0)]
    unnamed x81 -> x142, local copies, waits for them, and re-layouts: 11.2 us -> 39.5 us
    reduce_sum x0 -> x30, other arithmetic: none -> 12.5 us  [by_axis(): array = jnp.sum(lax.all_gather(array, axis), axis=0)]
  transfers between devices with their start and end apart: 24 -> 24, of which waited for: 7 -> 7; matrix products, arithmetic and copies ran while one was open for 34% -> 32% of each run, Pallas kernels for 0% -> 0%
where the time goes in v1:
time: 1000 us; the launch traced here: 992 us
  blocking collectives  282 us (28%)
  local copies, waits for them, and re-layouts  267 us (27%)
  other arithmetic  258 us (26%)
  matrix products  88.4 us (9%)
  starting transfers between devices  72 us (7%)
  waiting for transfers between devices  13.7 us (1%)
  between operations  10.9 us (1%)
    unnamed x12, blocking collectives  209 us
    gather x19, local copies, waits for them, and re-layouts, reorder(): return jnp.take_along_axis(values, positions, axis=-1)  185 us
    another operation x14, other arithmetic, invert(): factor_low = jnp.linalg.cholesky(summed)  145 us
    another operation x5, other arithmetic, invert(): lax.linalg.triangular_solve(factor_low, identity, left_side=True, lower=T...  85.3 us
    all_gather x10, blocking collectives, by_axis(): array = jnp.sum(lax.all_gather(array, axis), axis=0)  72.6 us
    ppermute x24, starting transfers between devices, from_behind(): lax.ppermute(value, axis, [(source, source + steps) for source in range(f...  72 us
    unnamed x142, local copies, waits for them, and re-layouts  39.5 us
  transfers between devices with their start and end apart: 24, of which 7 were waited for; matrix products, arithmetic and copies ran while one was open for 32% of the time, Pallas kernels for 0%

profile of v1, /device:TPU:1, one launch (start us, length us, event | category | flops | bytes accessed | tf_op | source)
XLA Modules:
  0.0 992.3 jit_solution(9871750573484048726)
XLA Ops:
  0.6 11.2 %reshape_reshape.3 = bf16[2,1536,4,256]{3,2,1,0:T(4,128)(2,1)} reshape(bf16[2,1,1536,1024]{3,2,1,0:T(8,128)(2,1)} %param.14) | data formatting | bytes 12582912 | tf_op jit(solution)/shard_map/reshape;reshape | solution.py:81
  11.9 16.5 %fusion.11 = bf16[2,1536,1024]{1,2,0:T(8,128)(2,1)} fusion(bf16[2,1,1536,1024]{3,2,1,0:T(8,128)(2,1)} %param.14, bf16[2,1,1536,1536]{3,2,1,0:T(8,128)(2,1)} %param.13), kind=kOutput, calls=%fused_computation.24 | convolution fusion | flops 9666822144 | bytes 22020096 | tf_op jit(solution)/shard_map/sij,sjk->sik/dot_general | solution.py:98
  28.9 6.4 fusion.20
  48.4 20.4 %gather_fusion = f32[2048]{0:T(1024)S(1)} fusion(f32[2,4,256]{2,1,0:T(4,128)S(1)} %bitcast.412, s32[2048]{0:T(1024)S(1)} %bitcast.419), kind=kCustom, calls=%fused_computation.clone | custom fusion | bytes 40960 | tf_op jit(solution)/shard_map/jit(take_along_axis)/gather | solution.py:34
  70.1 6.3 collective-permute-start
  104.8 23.5 %custom-call.36 = f32[2,128,128]{2,1,0:T(8,128)S(1)} custom-call(f32[2,128,128]{2,1,0:T(8,128)S(1)} %cholesky.198), custom_call_target="Cholesky" | custom-call | tf_op jit(solution)/shard_map/jit(cholesky)/cholesky | solution.py:46
  136.1 24.3 %custom-call.40 = f32[2,128,128]{2,1,0:T(8,128)S(1)} custom-call(f32[2,128,128]{2,1,0:T(8,128)} %cholesky.201), custom_call_target="Cholesky" | custom-call | tf_op jit(solution)/shard_map/jit(cholesky)/cholesky | solution.py:46
  161.8 21.1 %custom-call.37 = f32[2,1,128,128]{2,3,1,0:T(8,128)} custom-call(f32[2,1,128,128]{3,2,1,0:T(8,128)} %get-tuple-element.99), custom_call_target="InvertDiagBlocksLowerTriangular" | custom-call | tf_op jit(solution)/shard_map/jit(cholesky)/cholesky | solution.py:46
  186.7 25.0 %custom-call.38 = f32[2,128,128]{2,1,0:T(8,128)} custom-call(f32[2,128,128]{2,1,0:T(8,128)} %convolution_subtract_fusion.2), custom_call_target="Cholesky" | custom-call | tf_op jit(solution)/shard_map/jit(cholesky)/cholesky | solution.py:46
  211.8 21.1 %custom-call.41 = f32[2,1,128,128]{2,3,1,0:T(8,128)} custom-call(f32[2,1,128,128]{3,2,1,0:T(8,128)} %get-tuple-element.100), custom_call_target="InvertDiagBlocksLowerTriangular" | custom-call | tf_op jit(solution)/shard_map/jit(cholesky)/cholesky | solution.py:46
  237.5 24.9 %custom-call.42 = f32[2,128,128]{2,1,0:T(8,128)} custom-call(f32[2,128,128]{2,1,0:T(8,128)} %slice_subtract_fusion), custom_call_target="Cholesky" | custom-call | tf_op jit(solution)/shard_map/jit(cholesky)/cholesky | solution.py:46
  268.3 8.6 while.4
  276.9 40.9 %custom-call.39 = f32[2,2,128,128]{2,3,1,0:T(8,128)} custom-call(f32[2,2,128,128]{3,2,1,0:T(8,128)} %bitcast.440), custom_call_target="InvertDiagBlocksLowerTriangular" | custom-call | tf_op jit(solution)/shard_map/triangular_solve/custom-call.0 | solution.py:48
  324.4 8.6 while.5
  333.0 40.7 %custom-call.43 = f32[2,2,128,128]{2,3,1,0:T(8,128)} custom-call(f32[2,2,128,128]{3,2,1,0:T(8,128)} %bitcast.441), custom_call_target="InvertDiagBlocksLowerTriangular" | custom-call | tf_op jit(solution)/shard_map/triangular_solve/custom-call.0 | solution.py:48
  382.6 6.4 collective-permute-start.5
  398.2 21.2 %gather_fusion.1 = bf16[2048]{0:T(1024)(128)(2,1)S(1)} fusion(bf16[2,4,256]{2,1,0:T(4,128)(2,1)S(1)} %bitcast.413, s32[2048]{0:T(1024)S(1)} %bitcast.415), kind=kCustom, calls=%fused_computation.1.clone | custom fusion | bytes 32768 | tf_op jit(solution)/shard_map/jit(take_along_axis)/gather | solution.py:34
  419.9 73.3 %all-reduce.21 = f32[1792]{0:T(1024)S(1)} all-reduce(f32[1792]{0:T(1024)S(1)} %convolution_reduce_fusion.1), channel_id=12, replica_groups=mesh['gx_0'=4,'gx_1'=2,'gy_0'=4,'gy_1'=2,'gy_2'=2] {'gx_0','gx_1','gy_0'..., use_global_device_ids=true, to_apply=%region_5.0.clone | all-reduce | flops 1792 | bytes 14336
  493.4 9.3 all-gather.10
  502.8 4.7 all-gather.11
  507.6 9.1 all-gather.12
  520.2 9.8 all-gather.14
  530.8 20.4 %gather_fusion.2 = f32[2048]{0:T(1024)S(1)} fusion(f32[2,4,256]{2,1,0:T(4,128)S(1)} %reshape.122, s32[2048]{0:T(1024)S(1)} %bitcast.422), kind=kCustom, calls=%fused_computation.2.clone | custom fusion | bytes 40960 | tf_op jit(solution)/shard_map/jit(take_along_axis)/gather | solution.py:34
  567.8 20.4 %gather_fusion.3 = bf16[2048]{0:T(1024)(128)(2,1)S(1)} fusion(f32[2,4,256]{2,1,0:T(4,128)S(1)} %bitcast_multiply_fusion.1, s32[2048]{0:T(1024)S(1)} %bitcast.416), kind=kCustom, calls=%fused_computation.3.clone | custom fusion | bytes 32768 | tf_op jit(solution)/shard_map/jit(take_along_axis)/gather | solution.py:34
  592.9 6.4 fusion.2
  600.7 20.4 %gather_fusion.4 = f32[2048]{0:T(1024)S(1)} fusion(f32[2,4,256]{2,1,0:T(4,128)S(1)} %bitcast_subtract_fusion.3, s32[2048]{0:T(1024)S(1)} %bitcast.420), kind=kCustom, calls=%fused_computation.4.clone | custom fusion | bytes 40960 | tf_op jit(solution)/shard_map/jit(take_along_axis)/gather | solution.py:34
  621.2 6.4 collective-permute-start.12
  639.9 10.9 %all-reduce.26 = (f32[4]{0:T(128)S(1)}, f32[4]{0:T(128)S(1)}) all-reduce(f32[4]{0:T(128)S(1)} %dynamic-update-slice.9, f32[4]{0:T(128)S(1)} %dynamic-update-slice.14), channel_id=1, replica_groups=mesh['gx_0'=4,'gx_1'=2,'gy_0'=4,'gy_1'=2,'gy_2'=2] {'gx_0'}, use_global_device_ids=true, to_apply=%add.1 | all-reduce | flops 8 | bytes 64
  655.3 5.3 all-reduce.32
  665.0 7.6 all-reduce.24
  677.1 4.8 all-reduce.30
  685.7 8.9 all-reduce.28
  702.5 20.8 %gather_fusion.5 = bf16[2048]{0:T(1024)(128)(2,1)S(1)} fusion(bf16[2,4,256]{2,1,0:T(4,128)(2,1)S(1)} %bitcast.414, s32[2048]{0:T(1024)S(1)} %bitcast.417), kind=kCustom, calls=%fused_computation.5.clone | custom fusion | bytes 32768 | tf_op jit(solution)/shard_map/jit(take_along_axis)/gather | solution.py:34
  723.7 61.9 %all-reduce.22 = f32[1792]{0:T(1024)S(1)} all-reduce(f32[1792]{0:T(1024)S(1)} %convolution_reduce_fusion), channel_id=13, replica_groups=mesh['gx_0'=4,'gx_1'=2,'gy_0'=4,'gy_1'=2,'gy_2'=2] {'gx_0','gx_1','gy_0'..., use_global_device_ids=true, to_apply=%region_23.0.clone | all-reduce | flops 1792 | bytes 14336
  785.9 9.1 all-gather.15
  795.0 4.7 all-gather.16
  799.8 9.1 all-gather.17
  812.3 10.1 %all-gather.19 = f32[2,1,1792]{2,1,0:T(1,128)S(1)} all-gather(f32[1,1,1792]{2,1,0:T(1,128)S(1)} %reshape.350), channel_id=11, replica_groups=mesh['gx_0'=4,'gx_1'=2,'gy_0'=4,'gy_1'=2,'gy_2'=2] {'gy_2'}, dimensions={0}, use_global_device_ids=true | all-gather | bytes 21504 | tf_op jit(solution)/shard_map/all_gather | solution.py:22
  823.3 20.4 %gather_fusion.6 = f32[2048]{0:T(1024)S(1)} fusion(f32[2,4,256]{2,1,0:T(4,128)S(1)} %reshape.125, s32[2048]{0:T(1024)S(1)} %bitcast.423), kind=kCustom, calls=%fused_computation.6.clone | custom fusion | bytes 40960 | tf_op jit(solution)/shard_map/jit(take_along_axis)/gather | solution.py:34
  860.8 20.4 %gather_fusion.7 = bf16[2048]{0:T(1024)(128)(2,1)S(1)} fusion(f32[2,4,256]{2,1,0:T(4,128)S(1)} %bitcast_multiply_fusion, s32[2048]{0:T(1024)S(1)} %bitcast.418), kind=kCustom, calls=%fused_computation.7.clone | custom fusion | bytes 32768 | tf_op jit(solution)/shard_map/jit(take_along_axis)/gather | solution.py:34
  886.0 6.4 fusion
  893.7 20.4 %gather_fusion.8 = f32[2048]{0:T(1024)S(1)} fusion(f32[2,4,256]{2,1,0:T(4,128)S(1)} %bitcast_subtract_fusion.2, s32[2048]{0:T(1024)S(1)} %bitcast.421), kind=kCustom, calls=%fused_computation.8.clone | custom fusion | bytes 40960 | tf_op jit(solution)/shard_map/jit(take_along_axis)/gather | solution.py:34
  914.2 6.4 collective-permute-start.20
  932.1 10.5 %all-reduce.25 = (f32[4]{0:T(128)S(1)}, f32[4]{0:T(128)S(1)}) all-reduce(f32[4]{0:T(128)S(1)} %dynamic-update-slice.19, f32[4]{0:T(128)S(1)} %dynamic-update-slice.24), channel_id=1, replica_groups=mesh['gx_0'=4,'gx_1'=2,'gy_0'=4,'gy_1'=2,'gy_2'=2] {'gx_0'}, use_global_device_ids=true, to_apply=%add.11 | all-reduce | flops 8 | bytes 64
  946.9 5.3 all-reduce.31
  956.0 7.7 all-reduce.23
  967.7 4.8 all-reduce.29
  976.3 8.5 all-reduce.27
  (399 shorter events, 227.6 us)
Async XLA Ops:
  0.6 492.5 %copy-start = (f32[1792,14]{0,1:T(8,128)S(1)}, f32[1792,14]{0,1:T(8,128)}, u32[]{:S(2)}) copy-start(f32[1792,14]{0,1:T(8,128)} %param.20) | copy-start | bytes 301060
  11.9 16.5 %copy-start.2 = (bf16[2,1,4,256,256]{4,3,2,1,0:T(8,128)(2,1)S(1)}, bf16[2,1,4,256,256]{4,3,2,1,0:T(8,128)(2,1)}, u32[]{:S(2)}) copy-start(bf16[2,1,4,256,256]{4,3,2,1,0:T(8,128)(2,1)} %param.15) | copy-start | bytes 3145732
  39.9 58.6 %collective-permute-start.4 = (f32[256,256]{0,1:T(8,128)}, f32[256,256]{0,1:T(8,128)}, u32[]{:S(2)}, u32[]{:S(2)}) collective-permute-start(f32[256,256]{0,1:T(8,128)} %bitcast.439), channel_id=1, source_target_pairs={{16,0},{32,16},{48,32},{64,48},{80,64},{96,80},{112,96},{17,1},{33... | collective-permute-start | bytes 786440 | tf_op jit(solution)/shard_map/ppermute | solution.py:17
  44.6 84.6 %collective-permute-start.6 = (f32[2,256,256]{1,2,0:T(8,128)}, f32[2,256,256]{1,2,0:T(8,128)}, u32[]{:S(2)}, u32[]{:S(2)}) collective-permute-start(f32[2,256,256]{1,2,0:T(8,128)} %bitcast.438), channel_id=1, source_target_pairs={{1,0},{2,1},{3,2},{4,3},{5,4},{6,5},{7,6},{8,7},{9,8},{10,9},{11,1... | collective-permute-start | bytes 1572872 | tf_op jit(solution)/shard_map/ppermute | solution.py:17
  48.4 20.5 %copy-start.19 = (s32[2,4,256]{2,1,0:T(4,128)}, s32[2,4,256]{2,1,0:T(4,128)S(1)}, u32[]{:S(2)}) copy-start(s32[2,4,256]{2,1,0:T(4,128)S(1)} %select_reduce_fusion) | copy-start | bytes 24580
  70.1 25.2 %collective-permute-start = (f32[256]{0:T(256)}, f32[256]{0:T(256)}, u32[]{:S(2)}, u32[]{:S(2)}) collective-permute-start(f32[256]{0:T(256)} %bitcast.3), channel_id=1, source_target_pairs={{0,16},{16,32},{32,48},{48,64},{64,80},{80,96},{96,112},{1,17},{17... | collective-permute-start | bytes 3080 | tf_op jit(solution)/shard_map/ppermute | solution.py:17
  76.4 312.6 %collective-permute-start.1 = (f32[256]{0:T(256)}, f32[256]{0:T(256)}, u32[]{:S(2)}, u32[]{:S(2)}) collective-permute-start(f32[256]{0:T(256)} %bitcast.7), channel_id=1, source_target_pairs={{16,0},{32,16},{48,32},{64,48},{80,64},{96,80},{112,96},{17,1},{33... | collective-permute-start | bytes 3080 | tf_op jit(solution)/shard_map/ppermute | solution.py:17
  78.3 311.4 %collective-permute-start.2 = (f32[2,256]{1,0:T(2,128)}, f32[2,256]{1,0:T(2,128)}, u32[]{:S(2)}, u32[]{:S(2)}) collective-permute-start(f32[2,256]{1,0:T(2,128)} %get-tuple-element.129), channel_id=1, source_target_pairs={{0,1},{1,2},{2,3},{3,4},{4,5},{5,6},{6,7},{7,8},{8,9},{9,10},{10,1... | collective-permute-start | bytes 6152 | tf_op jit(solution)/shard_map/ppermute | solution.py:17
  95.3 295.0 %collective-permute-start.3 = (f32[2,256]{1,0:T(2,128)}, f32[2,256]{1,0:T(2,128)}, u32[]{:S(2)}, u32[]{:S(2)}) collective-permute-start(f32[2,256]{1,0:T(2,128)} %get-tuple-element.130), channel_id=1, source_target_pairs={{1,0},{2,1},{3,2},{4,3},{5,4},{6,5},{7,6},{8,7},{9,8},{10,9},{11,1... | collective-permute-start | bytes 6152 | tf_op jit(solution)/shard_map/ppermute | solution.py:17
  264.2 53.6 %copy-start.9 = (f32[128,256]{1,0:T(8,128)S(1)}, f32[128,256]{1,0:T(8,128)}, u32[]{:S(2)}) copy-start(f32[128,256]{1,0:T(8,128)} %get-tuple-element.94) | copy-start | bytes 393220
  264.5 54.6 %copy-start.8 = (f32[128,256]{1,0:T(8,128)S(1)}, f32[128,256]{1,0:T(8,128)}, u32[]{:S(2)}) copy-start(f32[128,256]{1,0:T(8,128)} %get-tuple-element.93) | copy-start | bytes 393220
  373.7 15.2 %copy-start.26 = (f32[1,256]{1,0:T(1,128)S(1)}, f32[1,256]{1,0:T(1,128)}, u32[]{:S(2)}) copy-start(f32[1,256]{1,0:T(1,128)} %get-tuple-element.127) | copy-start | bytes 3076
  373.7 15.9 %copy-start.25 = (f32[2,256]{1,0:T(2,128)S(1)}, f32[2,256]{1,0:T(2,128)}, u32[]{:S(2)}) copy-start(f32[2,256]{1,0:T(2,128)} %pad_maximum_fusion.1) | copy-start | bytes 6148
  373.7 17.2 %copy-start.21 = (f32[2,4]{1,0:T(2,128)S(1)}, f32[2,4]{1,0:T(2,128)}, u32[]{:S(2)}) copy-start(f32[2,4]{1,0:T(2,128)} %add_convert_fusion) | copy-start | bytes 100
  378.8 17.4 %copy-start.10 = (f32[2,256,256]{2,1,0:T(8,128)}, f32[2,256,256]{2,1,0:T(8,128)S(1)}, u32[]{:S(2)}) copy-start(f32[2,256,256]{2,1,0:T(8,128)S(1)} %fusion.44) | copy-start | bytes 1572868
  378.8 15.5 %collective-permute-start.7 = (f32[2,256,256]{2,1,0:T(8,128)S(1)}, f32[2,256,256]{2,1,0:T(8,128)S(1)}, u32[]{:S(2)}, u32[]{:S(2)}) collective-permute-start(f32[2,256,256]{2,1,0:T(8,128)S(1)} %fusion.44), channel_id=1, source_target_pairs={{0,1},{1,2},{2,3},{3,4},{4,5},{5,6},{6,7},{7,8},{8,9},{9,10},{10,1... | collective-permute-start | bytes 1572872 | tf_op jit(solution)/shard_map/ppermute | solution.py:17
  382.6 11.7 %collective-permute-start.5 = (f32[256,256]{1,0:T(8,128)S(1)}, f32[256,256]{1,0:T(8,128)S(1)}, u32[]{:S(2)}, u32[]{:S(2)}) collective-permute-start(f32[256,256]{1,0:T(8,128)S(1)} %get-tuple-element.91), channel_id=1, source_target_pairs={{0,16},{16,32},{32,48},{48,64},{64,80},{80,96},{96,112},{1,17},{17... | collective-permute-start | bytes 786440 | tf_op jit(solution)/shard_map/ppermute | solution.py:17
  398.1 21.2 %copy-start.18 = (s32[2,1,4,256]{3,2,1,0:T(4,128)S(1)}, s32[2,1,4,256]{3,2,1,0:T(4,128)}, u32[]{:S(2)}) copy-start(s32[2,1,4,256]{3,2,1,0:T(4,128)} %param.18) | copy-start | bytes 24580
  398.2 21.3 %copy-start.16 = (bf16[2,1,24,1024]{3,2,1,0:T(8,128)(2,1)S(1)}, bf16[2,1,24,1024]{3,2,1,0:T(8,128)(2,1)}, u32[]{:S(2)}) copy-start(bf16[2,1,24,1024]{3,2,1,0:T(8,128)(2,1)} %param.16) | copy-start | bytes 294916
  398.2 21.4 %copy-start.30 = (s32[2,1,24]{2,1,0:T(1,128)S(1)}, s32[2,1,24]{2,1,0:T(1,128)}, u32[]{:S(2)}) copy-start(s32[2,1,24]{2,1,0:T(1,128)} %param.19) | copy-start | bytes 580
  530.8 20.5 %copy-start.20 = (s32[2,4,256]{2,1,0:T(4,128)S(1)}, s32[2,4,256]{2,1,0:T(4,128)}, u32[]{:S(2)}) copy-start(s32[2,4,256]{2,1,0:T(4,128)} %copy-done.19) | copy-start | bytes 24580
  551.3 14.6 %copy-start.4 = (f32[2,256,256]{2,1,0:T(8,128)S(1)}, f32[2,256,256]{2,1,0:T(8,128)}, u32[]{:S(2)}) copy-start(f32[2,256,256]{2,1,0:T(8,128)} %fusion.40) | copy-start | bytes 1572868
  551.3 14.5 %copy-start.11 = (f32[2,256,256]{2,1,0:T(8,128)S(1)}, f32[2,256,256]{2,1,0:T(8,128)}, u32[]{:S(2)}) copy-start(f32[2,256,256]{2,1,0:T(8,128)} %copy-done.10) | copy-start | bytes 1572868
  553.2 9.6 collective-permute-start.8
  557.0 5.8 collective-permute-start.9
  558.3 4.6 collective-permute-start.10
  560.9 4.9 collective-permute-start.11
  600.6 20.5 %copy-start.23 = (pred[2,4,256]{2,0,1:T(4,128)(4,1)S(1)}, pred[2,4,256]{2,0,1:T(4,128)(4,1)}, u32[]{:S(2)}) copy-start(pred[2,4,256]{2,0,1:T(4,128)(4,1)} %get-tuple-element.81) | copy-start | bytes 6148
  600.6 38.7 %copy-start.34 = (u32[128]{0:T(128)S(1)}, u32[128]{0:T(128)}, u32[]{:S(2)}) copy-start(u32[128]{0:T(128)} %constant.310) | copy-start | bytes 1540
  600.6 54.1 %copy-start.33 = (u32[128]{0:T(128)S(1)}, u32[128]{0:T(128)}, u32[]{:S(2)}) copy-start(u32[128]{0:T(128)} %constant.315) | copy-start | bytes 1540
  600.7 63.8 %copy-start.32 = (u32[128]{0:T(128)S(1)}, u32[128]{0:T(128)}, u32[]{:S(2)}) copy-start(u32[128]{0:T(128)} %constant.320) | copy-start | bytes 1540
  600.7 75.9 %copy-start.31 = (u32[128]{0:T(128)S(1)}, u32[128]{0:T(128)}, u32[]{:S(2)}) copy-start(u32[128]{0:T(128)} %constant.325) | copy-start | bytes 1540
  621.2 12.0 %collective-permute-start.12 = (f32[256]{0:T(256)S(1)}, f32[256]{0:T(256)S(1)}, u32[]{:S(2)}, u32[]{:S(2)}) collective-permute-start(f32[256]{0:T(256)S(1)} %bitcast.481), channel_id=1, source_target_pairs={{0,16},{16,32},{32,48},{48,64},{64,80},{80,96},{96,112},{1,17},{17... | collective-permute-start | bytes 3080 | tf_op jit(solution)/shard_map/ppermute | solution.py:17
  627.6 5.8 collective-permute-start.13
  628.9 4.5 collective-permute-start.14
  630.8 4.9 collective-permute-start.15
  843.7 15.2 %copy-start.5 = (f32[2,256,256]{2,1,0:T(8,128)S(1)}, f32[2,256,256]{2,1,0:T(8,128)}, u32[]{:S(2)}) copy-start(f32[2,256,256]{2,1,0:T(8,128)} %fusion.40) | copy-start | bytes 1572868
  843.7 15.2 %copy-start.12 = (f32[2,256,256]{2,1,0:T(8,128)S(1)}, f32[2,256,256]{2,1,0:T(8,128)}, u32[]{:S(2)}) copy-start(f32[2,256,256]{2,1,0:T(8,128)} %copy-done.10) | copy-start | bytes 1572868
  843.7 15.2 %copy-start.15 = (f32[2,1,256,256]{3,2,0,1:T(8,128)S(1)}, f32[2,1,256,256]{3,2,0,1:T(8,128)}, u32[]{:S(2)}) copy-start(f32[2,1,256,256]{3,2,0,1:T(8,128)} %copy-done.13) | copy-start | bytes 1572868
  843.8 15.2 %copy-start.29 = (f32[2,256,256]{2,1,0:T(8,128)S(1)}, f32[2,256,256]{2,1,0:T(8,128)}, u32[]{:S(2)}) copy-start(f32[2,256,256]{2,1,0:T(8,128)} %copy-done.27) | copy-start | bytes 1572868
  845.7 10.4 %collective-permute-start.16 = (f32[256]{0:T(256)S(1)}, f32[256]{0:T(256)S(1)}, u32[]{:S(2)}, u32[]{:S(2)}) collective-permute-start(f32[256]{0:T(256)S(1)} %bitcast.482), channel_id=1, source_target_pairs={{0,16},{16,32},{32,48},{48,64},{64,80},{80,96},{96,112},{1,17},{17... | collective-permute-start | bytes 3080 | tf_op jit(solution)/shard_map/ppermute | solution.py:17
  849.1 7.1 collective-permute-start.17
  850.4 5.8 collective-permute-start.18
  853.9 4.9 collective-permute-start.19
  914.2 12.0 %collective-permute-start.20 = (f32[256]{0:T(256)S(1)}, f32[256]{0:T(256)S(1)}, u32[]{:S(2)}, u32[]{:S(2)}) collective-permute-start(f32[256]{0:T(256)S(1)} %bitcast.483), channel_id=1, source_target_pairs={{0,16},{16,32},{32,48},{48,64},{64,80},{80,96},{96,112},{1,17},{17... | collective-permute-start | bytes 3080 | tf_op jit(solution)/shard_map/ppermute | solution.py:17
  920.5 5.8 collective-permute-start.21
  921.8 4.5 collective-permute-start.22
  923.8 4.9 collective-permute-start.23
  (16 other events, 121.5 us)
